TPU v7x, 32 devices: a whole 2x2x4 slice. The times are simulated.
32 devices in a mesh: sec: 4 (over z), blk: 8 (over y, x, core).
Axes of the slice: x: 2, y: 2, z: 4, core: 2. Of those that a mesh axis runs over, the one named last changes fastest.
Arguments:
- raw: bfloat16 [32, 128, 256], P(('sec', 'blk')), may hold values from -6 to 6
- tissue: int32 [4, 8, 4], P('sec', 'blk'), may hold values 0 or 1
- w_emb: bfloat16 [32, 3, 3], replicated, may hold values from -3 to 3
- w_one: bfloat16 [32, 32, 3, 3], replicated, may hold values from -0.5 to 0.5
- w_down: bfloat16 [64, 32, 2, 2], replicated, may hold values from -0.75 to 0.75
- w_deep: bfloat16 [64, 64, 3, 3, 3], replicated, may hold values from -0.21875 to 0.21875
- w_up: bfloat16 [32, 64, 2, 2], replicated, may hold values from -1 to 1
- w_out: bfloat16 [3, 32], replicated, may hold values from -1 to 1
Outputs:
- logits: float32 [3, 32, 128, 256], P(None, 'sec', 'blk')
Inputs may be any that keep to these rules, and one draw needn't show every extreme that they name: 1 marks a block of 8 sections, 16 columns and one 4-th of the rows that holds tissue, 0 one without.
All inputs are finite; a program needn't handle non-finite values.
Results may differ from a plain program's by a relative error of at most 0.0067.
Values may be sent and summed in bfloat16 or wider, within the bound.
A program may use at most 256 MiB of HBM per device.

v0:
```python
import jax
import jax.numpy as jnp
from jax import lax
from jax.sharding import PartitionSpec as P


def extended(value, sides, width):
    for axis, dim in sides:
        peers, length = (lax.axis_size(axis), value.shape[dim])
        up = [(i, (i + 1) % peers) for i in range(peers - 1)]
        down = [(j, i) for i, j in up]
        last = lax.slice_in_dim(value, length - width, length, axis=dim)
        leading = lax.slice_in_dim(value, 0, width, axis=dim)
        before = lax.ppermute(last, axis, up)
        after = lax.ppermute(leading, axis, down)
        value = jnp.concatenate([before, value, after], axis=dim)
    return value


def embed(padded, w_emb, columns_out, length_y):
    stacked = []
    for offset_x in range(3):
        for offset_y in range(3):
            stacked.append(
                padded[:, offset_x : offset_x + columns_out, offset_y : offset_y + length_y]
            )
    stacked = jnp.stack(stacked, 0)
    weights = w_emb.reshape(w_emb.shape[0], 9)
    summed = jnp.einsum("ck,kzxy->czxy", weights, stacked, preferred_element_type=jnp.float32)
    return jnp.maximum(summed, 0.0).astype(jnp.bfloat16)


def conv_plane(padded, weights, width_x, length_y):
    summed = None
    for offset_x in range(3):
        for offset_y in range(3):
            window = padded[:, :, offset_x : offset_x + width_x, offset_y : offset_y + length_y]
            contribution = jnp.einsum(
                "oc,czxy->ozxy",
                weights[:, :, offset_x, offset_y],
                window,
                preferred_element_type=jnp.float32,
            )
            summed = contribution if summed is None else summed + contribution
    return summed


def conv_volume(padded, weights, depth_z, width_x, length_y):
    summed = None
    for offset_z in range(3):
        for offset_x in range(3):
            for offset_y in range(3):
                window = padded[
                    :,
                    offset_z : offset_z + depth_z,
                    offset_x : offset_x + width_x,
                    offset_y : offset_y + length_y,
                ]
                contribution = jnp.einsum(
                    "oc,czxy->ozxy",
                    weights[:, :, offset_z, offset_x, offset_y],
                    window,
                    preferred_element_type=jnp.float32,
                )
                summed = contribution if summed is None else summed + contribution
    return summed


def per_device(raw, tissue, w_emb, w_one, w_down, w_deep, w_up, w_out):
    sections = lax.all_to_all(raw, "blk", split_axis=1, concat_axis=0, tiled=True)
    depth_z, width_x, length_y = sections.shape
    blocks_y = tissue.shape[2]
    span_y = length_y // blocks_y
    half_x = width_x // 2
    half_y = length_y // 2
    half_span = span_y // 2
    channels = w_emb.shape[0]
    flags = tissue[0, 0].astype(jnp.float32)
    mask_full = jnp.repeat(flags, span_y)
    mask_half = jnp.repeat(flags, half_span)
    masked = sections * mask_full.astype(jnp.bfloat16)
    narrow = extended(masked, (("blk", 1),), 1)
    narrow = jnp.pad(narrow, ((0, 0), (0, 0), (1, 1)))
    local_emb = embed(narrow, w_emb, width_x, length_y)
    embedded = extended(local_emb, (("blk", 2),), 1)
    embedded = jnp.pad(embedded, ((0, 0), (0, 0), (0, 0), (1, 1)))
    first_sum = conv_plane(embedded, w_one, width_x, length_y)
    features = (jnp.maximum(first_sum, 0.0) * mask_full).astype(jnp.bfloat16)
    shaped = features.reshape(channels, depth_z, half_x, 2, half_y, 2)
    lowered = jnp.einsum("ocab,czxayb->ozxy", w_down, shaped, preferred_element_type=jnp.float32)
    down = (jnp.maximum(lowered, 0.0) * mask_half).astype(jnp.bfloat16)
    rimmed = extended(down, (("sec", 1), ("blk", 2)), 1)
    rimmed = jnp.pad(rimmed, ((0, 0), (0, 0), (0, 0), (1, 1)))
    deep_sum = conv_volume(rimmed, w_deep, depth_z, half_x, half_y)
    deep = (jnp.maximum(deep_sum, 0.0) * mask_half).astype(jnp.bfloat16)
    raised = jnp.einsum("ocab,czxy->ozxayb", w_up, deep, preferred_element_type=jnp.float32)
    raised = raised.reshape(channels, depth_z, width_x, length_y)
    decoded = (jnp.maximum(raised + features.astype(jnp.float32), 0.0) * mask_full).astype(
        jnp.bfloat16
    )
    logits = jnp.einsum("oc,czxy->ozxy", w_out, decoded, preferred_element_type=jnp.float32)
    return logits * mask_full


def solution(mesh):
    placed = (P(("sec", "blk"), None, None), P("sec", "blk", None), P(), P(), P(), P(), P(), P())
    return jax.shard_map(
        per_device,
        mesh=mesh,
        in_specs=placed,
        out_specs=P(None, "sec", "blk", None),
        check_vma=False,
    )
```

profile of v0, /device:TPU:11, one launch (start us, length us, event | category | flops | bytes accessed | tf_op | source)
XLA Modules:
  0.0 189.1 jit_solution(16628197516298694183)
XLA Ops:
  3.1 4.6 %all-to-all-start = ((bf16[8,2,2048]{2,1,0:T(2,128)(2,1)}), bf16[8,2,2048]{2,1,0:T(2,128)(2,1)S(1)}, u32[]{:S(2)}, u32[]{:S(2)}) async-start(bf16[8,2,2048]{2,1,0:T(2,128)(2,1)} %reshape.77), calls=%async_computation | async-start | bytes 131072 | tf_op jit(solution)/shard_map/all_to_all | solution.py:70
  11.2 3.5 %collective-permute-start = (bf16[8,1,256]{2,1,0:T(2,128)(2,1)S(1)}, bf16[8,1,256]{2,1,0:T(2,128)(2,1)S(1)}, u32[]{:S(2)}, u32[]{:S(2)}) collective-permute-start(bf16[8,1,256]{2,1,0:T(2,128)(2,1)S(1)} %get-tuple-element.21), channel_id=1, source_target_pairs={{0,1},{1,2},{2,3},{3,4},{4,5},{5,6},{6,7},{8,9},{9,10},{10,11},{11... | collective-permute-start | bytes 12296 | tf_op jit(solution)/shard_map/ppermute | solution.py:14
  16.8 3.8 %collective-permute-done.1 = bf16[8,1,256]{2,1,0:T(2,128)(2,1)S(1)} collective-permute-done((bf16[8,1,256]{2,1,0:T(2,128)(2,1)S(1)}, bf16[8,1,256]{2,1,0:T(2,128)(2,1)S(1)}, u32[]{:S(2)}, u32[]{:S(2)}) %collective-permute-start.1) | collective-permute-done | bytes 4128 | tf_op jit(solution)/shard_map/ppermute | solution.py:15
  26.5 2.6 %collective-permute-start.3 = (bf16[32,8,1,256]{3,0,2,1:T(8,128)(2,1)S(1)}, bf16[32,8,1,256]{3,0,2,1:T(8,128)(2,1)S(1)}, u32[]{:S(2)}, u32[]{:S(2)}) collective-permute-start(bf16[32,8,1,256]{3,0,2,1:T(8,128)(2,1)S(1)} %get-tuple-element.6), channel_id=1, source_target_pairs={{1,0},{2,1},{3,2},{4,3},{5,4},{6,5},{7,6},{9,8},{10,9},{11,10},{12... | collective-permute-start | bytes 393224 | tf_op jit(solution)/shard_map/ppermute | solution.py:15
  29.1 2.6 %fusion.175 = f32[8,16,256,32]{2,3,1,0:T(8,128)} fusion(bf16[32,8,16,256]{3,0,2,1:T(8,128)(2,1)S(1)} %fusion.41, bf16[32,32,3,3]{1,0,3,2:T(8,128)(2,1)S(1)} %copy-done.4), kind=kOutput, calls=%fused_computation.206 | convolution fusion | flops 67108864 | bytes 6299648 | tf_op jit(solution)/shard_map/oc,czxy->ozxy/dot_general | solution.py:38
  33.7 2.4 %fusion.8 = bf16[32,8,18,258]{3,0,2,1:T(8,128)(2,1)S(1)} fusion(bf16[32,8,1,256]{3,0,2,1:T(8,128)(2,1)S(1)} %collective-permute-done.3, bf16[32,8,16,256]{3,0,2,1:T(8,128)(2,1)S(1)} %fusion.41, bf16[32,8,1,256]{3,0,2,1:T(8,128)(2,1)S(1)} %collective-permute-done.2), kind=kLoop, calls=%fused_computation.15 | loop fusion | flops 14266368 | bytes 4737024 | tf_op jit(solution)/shard_map/concatenate | solution.py:16
  36.1 2.7 %fusion.20 = f32[8,16,256,32]{2,3,1,0:T(8,128)} fusion(bf16[32,8,18,258]{3,0,2,1:T(8,128)(2,1)S(1)} %fusion.8, bf16[32,32,3,3]{1,0,3,2:T(8,128)(2,1)S(1)} %copy-done.4), kind=kOutput, calls=%fused_computation.29 | convolution fusion | flops 67108864 | bytes 6299648 | tf_op jit(solution)/shard_map/oc,czxy->ozxy/dot_general | solution.py:38
  38.7 2.8 %fusion.22 = f32[8,16,256,32]{2,3,1,0:T(8,128)} fusion(bf16[32,8,18,258]{3,0,2,1:T(8,128)(2,1)S(1)} %fusion.8, bf16[32,32,3,3]{1,0,3,2:T(8,128)(2,1)S(1)} %copy-done.4), kind=kOutput, calls=%fused_computation.31 | convolution fusion | flops 67108864 | bytes 6299648 | tf_op jit(solution)/shard_map/oc,czxy->ozxy/dot_general | solution.py:38
  41.5 2.6 %fusion.24 = f32[8,16,256,32]{2,3,1,0:T(8,128)} fusion(bf16[32,8,18,258]{3,0,2,1:T(8,128)(2,1)S(1)} %fusion.8, bf16[32,32,3,3]{1,0,3,2:T(8,128)(2,1)S(1)} %copy-done.4), kind=kOutput, calls=%fused_computation.33 | convolution fusion | flops 67108864 | bytes 6299648 | tf_op jit(solution)/shard_map/oc,czxy->ozxy/dot_general | solution.py:38
  44.1 2.8 %fusion.26 = f32[8,16,256,32]{2,3,1,0:T(8,128)} fusion(bf16[32,8,18,258]{3,0,2,1:T(8,128)(2,1)S(1)} %fusion.8, bf16[32,32,3,3]{1,0,3,2:T(8,128)(2,1)S(1)} %copy-done.4), kind=kOutput, calls=%fused_computation.35 | convolution fusion | flops 67108864 | bytes 6299648 | tf_op jit(solution)/shard_map/oc,czxy->ozxy/dot_general | solution.py:38
  46.9 2.7 %fusion.30 = f32[8,16,256,32]{2,3,1,0:T(8,128)} fusion(bf16[32,8,18,258]{3,0,2,1:T(8,128)(2,1)S(1)} %fusion.8, bf16[32,32,3,3]{1,0,3,2:T(8,128)(2,1)S(1)} %copy-done.4), kind=kOutput, calls=%fused_computation.40 | convolution fusion | flops 67108864 | bytes 6299648 | tf_op jit(solution)/shard_map/oc,czxy->ozxy/dot_general | solution.py:38
  50.3 2.6 %fusion.18 = f32[8,16,256,32]{2,3,1,0:T(8,128)} fusion(bf16[32,8,1,256]{3,0,2,1:T(8,128)(2,1)S(1)} %collective-permute-done.3, bf16[32,8,16,256]{3,0,2,1:T(8,128)(2,1)S(1)} %fusion.41, bf16[32,32,3,3]{1,0,3,2:T(8,128)(2,1)S(1)} %copy-done.4), kind=kOutput, calls=%fused_computation.27 | convolution fusion | flops 71303168 | bytes 6430720 | tf_op jit(solution)/shard_map/oc,czxy->ozxy/dot_general | solution.py:38
  52.9 10.9 %fusion.38 = bf16[32,8,16,256]{3,0,2,1:T(8,128)(2,1)S(1)} fusion(f32[256]{0:T(256)S(1)} %reshape.30, bf16[32,8,18,258]{3,0,2,1:T(8,128)(2,1)S(1)} %fusion.8, f32[8,16,256,32]{2,3,1,0:T(8,128)} %fusion.18, f32[8,16,256,32]{2,3,1,0:T(8,128)} %fusion.20, f32[8,16,256,32]{2,3,1,0:T(8,128)} %fusion.22, f32[8,16,256,32]{2,3,1,0:T(8,128)} %fusion.175, ...), kind=kOutput, calls=%fused_computation.59 | convolution fusion | flops 78643200 | bytes 37757952 | tf_op jit(solution)/shard_map/oc,czxy->ozxy/dot_general | solution.py:38
  63.9 6.7 %copy.169 = bf16[32,8,16,256]{0,1,3,2:T(8,128)(2,1)} copy(bf16[32,8,16,256]{3,0,2,1:T(8,128)(2,1)S(1)} %fusion.38) | data formatting | bytes 4194304 | tf_op jit(solution)/shard_map/convert_element_type | solution.py:88
  70.5 6.3 %fusion.45 = bf16[64,8,8,128]{3,0,2,1:T(8,128)(2,1)S(1)} fusion(bf16[32,8,8,2,128,2]{0,1,5,4,3,2:T(8,128)(2,1)} %bitcast.394, f32[128]{0:T(128)S(1)} %mul.67, bf16[64,32,2,2,1,1]{0,3,2,1,5,4:T(2,128)(2,1)S(1)} %bitcast.399), kind=kOutput, calls=%fused_computation.64 | convolution fusion | flops 135790592 | bytes 3162624 | tf_op jit(solution)/shard_map/ocab,czxayb->ozxy/dot_general | solution.py:90
  76.8 3.2 %collective-permute-start.4 = (bf16[64,1,8,128]{3,0,2,1:T(8,128)(2,1)S(1)}, bf16[64,1,8,128]{3,0,2,1:T(8,128)(2,1)S(1)}, u32[]{:S(2)}, u32[]{:S(2)}) collective-permute-start(bf16[64,1,8,128]{3,0,2,1:T(8,128)(2,1)S(1)} %get-tuple-element.11), channel_id=1, source_target_pairs={{0,8},{8,16},{16,24},{1,9},{9,17},{17,25},{2,10},{10,18},{18,26},{... | collective-permute-start | bytes 393224 | tf_op jit(solution)/shard_map/ppermute | solution.py:14
  83.9 2.1 %collective-permute-done.5 = bf16[64,1,8,128]{3,0,2,1:T(8,128)(2,1)S(1)} collective-permute-done((bf16[64,1,8,128]{3,0,2,1:T(8,128)(2,1)S(1)}, bf16[64,1,8,128]{3,0,2,1:T(8,128)(2,1)S(1)}, u32[]{:S(2)}, u32[]{:S(2)}) %collective-permute-start.5) | collective-permute-done | bytes 131104 | tf_op jit(solution)/shard_map/ppermute | solution.py:15
  86.0 3.4 %collective-permute-start.6 = (bf16[64,10,1,128]{3,0,2,1:T(8,128)(2,1)S(1)}, bf16[64,10,1,128]{3,0,2,1:T(8,128)(2,1)S(1)}, u32[]{:S(2)}, u32[]{:S(2)}) collective-permute-start(bf16[64,10,1,128]{3,0,2,1:T(8,128)(2,1)S(1)} %get-tuple-element.9), channel_id=1, source_target_pairs={{0,1},{1,2},{2,3},{3,4},{4,5},{5,6},{6,7},{8,9},{9,10},{10,11},{11... | collective-permute-start | bytes 491528 | tf_op jit(solution)/shard_map/ppermute | solution.py:14
  94.8 2.1 %collective-permute-done.7 = bf16[64,10,1,128]{3,0,2,1:T(8,128)(2,1)S(1)} collective-permute-done((bf16[64,10,1,128]{3,0,2,1:T(8,128)(2,1)S(1)}, bf16[64,10,1,128]{3,0,2,1:T(8,128)(2,1)S(1)}, u32[]{:S(2)}, u32[]{:S(2)}) %collective-permute-start.7) | collective-permute-done | bytes 163872 | tf_op jit(solution)/shard_map/ppermute | solution.py:15
  96.9 3.1 %select_maximum_fusion = bf16[64,10,10,130]{3,0,2,1:T(8,128)(2,1)S(1)} fusion(bf16[64,10,1,128]{3,0,2,1:T(8,128)(2,1)S(1)} %collective-permute-done.7, bf16[64,10,1,128]{3,0,2,1:T(8,128)(2,1)S(1)} %collective-permute-done.6, bf16[64,1,8,128]{3,0,2,1:T(8,128)(2,1)S(1)} %collective-permute-done.5, bf16[64,8,8,128]{3,0,2,1:T(8,128)(2,1)S(1)} %fusion.45, ...), kind=kLoop, calls=%fused_computation.16 | loop fusion | flops 14976000 | bytes 3302400 | tf_op jit(solution)/shard_map/concatenate | solution.py:16
  141.9 20.8 %convolution_bitcast_fusion = f32[32,8,8,2,128,2]{4,0,5,3,2,1:T(8,128)} fusion(f32[8,8,128,64]{2,3,1,0:T(8,128)} %fusion.52, f32[8,8,128,64]{2,3,1,0:T(8,128)} %fusion.54, f32[8,8,128,64]{2,3,1,0:T(8,128)} %fusion.56, f32[8,8,128,64]{2,3,1,0:T(8,128)} %fusion.58, f32[8,8,128,64]{2,3,1,0:T(8,128)} %fusion.60, f32[8,8,128,64]{2,3,1,0:T(8,128)} %fusion.62, ...), kind=kOutput, calls=%fused_computation.23 | convolution fusion | flops 216530944 | bytes 59818496 | tf_op jit(solution)/shard_map/ocab,czxy->ozxayb/dot_general | solution.py:96
  162.8 11.0 %copy.173 = f32[32,8,8,2,128,2]{0,1,5,4,3,2:T(8,128)} copy(f32[32,8,8,2,128,2]{4,0,5,3,2,1:T(8,128)} %convolution_bitcast_fusion) | data formatting | bytes 8388608 | tf_op jit(solution)/shard_map/ocab,czxy->ozxayb/transpose | solution.py:96
  173.7 11.5 %copy.174 = f32[32,8,16,256]{3,0,2,1:T(8,128)} copy(f32[32,8,16,256]{0,1,3,2:T(8,128)} %bitcast.393) | data formatting | bytes 8388608 | tf_op jit(solution)/shard_map/reshape | solution.py:97
  185.3 2.9 %fusion.49 = f32[3,8,16,256]{3,0,2,1:T(4,128)S(1)} fusion(f32[32,8,16,256]{3,0,2,1:T(8,128)} %copy.174, bf16[32,8,16,256]{3,0,2,1:T(8,128)(2,1)S(1)} %copy-done.2, f32[256]{0:T(256)S(1)} %reshape.30, bf16[3,32]{1,0:T(4,128)(2,1)S(1)} %copy-done.5), kind=kOutput, calls=%fused_computation.66 | convolution fusion | flops 11632640 | bytes 6685888 | tf_op jit(solution)/shard_map/oc,czxy->ozxy/dot_general | solution.py:101
  (85 shorter events, 69.1 us)
Async XLA Ops:
  0.0 141.9 %copy-start = (bf16[32,64,2,2]{1,3,2,0:T(2,128)(2,1)S(1)}, bf16[32,64,2,2]{1,3,2,0:T(2,128)(2,1)}, u32[]{:S(2)}) copy-start(bf16[32,64,2,2]{1,3,2,0:T(2,128)(2,1)} %param.14) | copy-start | bytes 49156
  3.1 7.9 %all-to-all-start = ((bf16[8,2,2048]{2,1,0:T(2,128)(2,1)}), bf16[8,2,2048]{2,1,0:T(2,128)(2,1)S(1)}, u32[]{:S(2)}, u32[]{:S(2)}) async-start(bf16[8,2,2048]{2,1,0:T(2,128)(2,1)} %reshape.77), calls=%async_computation | async-start | bytes 131072 | tf_op jit(solution)/shard_map/all_to_all | solution.py:70
  11.2 5.6 %collective-permute-start = (bf16[8,1,256]{2,1,0:T(2,128)(2,1)S(1)}, bf16[8,1,256]{2,1,0:T(2,128)(2,1)S(1)}, u32[]{:S(2)}, u32[]{:S(2)}) collective-permute-start(bf16[8,1,256]{2,1,0:T(2,128)(2,1)S(1)} %get-tuple-element.21), channel_id=1, source_target_pairs={{0,1},{1,2},{2,3},{3,4},{4,5},{5,6},{6,7},{8,9},{9,10},{10,11},{11... | collective-permute-start | bytes 12296 | tf_op jit(solution)/shard_map/ppermute | solution.py:14
  14.7 5.9 %collective-permute-start.1 = (bf16[8,1,256]{2,1,0:T(2,128)(2,1)S(1)}, bf16[8,1,256]{2,1,0:T(2,128)(2,1)S(1)}, u32[]{:S(2)}, u32[]{:S(2)}) collective-permute-start(bf16[8,1,256]{2,1,0:T(2,128)(2,1)S(1)} %get-tuple-element.22), channel_id=1, source_target_pairs={{1,0},{2,1},{3,2},{4,3},{5,4},{6,5},{7,6},{9,8},{10,9},{11,10},{12... | collective-permute-start | bytes 12296 | tf_op jit(solution)/shard_map/ppermute | solution.py:15
  23.7 5.3 %copy-start.4 = (bf16[32,32,3,3]{1,0,3,2:T(8,128)(2,1)S(1)}, bf16[32,32,3,3]{1,0,3,2:T(8,128)(2,1)}, u32[]{:S(2)}) copy-start(bf16[32,32,3,3]{1,0,3,2:T(8,128)(2,1)} %param.11) | copy-start | bytes 55300
  24.5 7.2 %collective-permute-start.2 = (bf16[32,8,1,256]{3,0,2,1:T(8,128)(2,1)S(1)}, bf16[32,8,1,256]{3,0,2,1:T(8,128)(2,1)S(1)}, u32[]{:S(2)}, u32[]{:S(2)}) collective-permute-start(bf16[32,8,1,256]{3,0,2,1:T(8,128)(2,1)S(1)} %get-tuple-element.5), channel_id=1, source_target_pairs={{0,1},{1,2},{2,3},{3,4},{4,5},{5,6},{6,7},{8,9},{9,10},{10,11},{11... | collective-permute-start | bytes 393224 | tf_op jit(solution)/shard_map/ppermute | solution.py:14
  26.5 7.2 %collective-permute-start.3 = (bf16[32,8,1,256]{3,0,2,1:T(8,128)(2,1)S(1)}, bf16[32,8,1,256]{3,0,2,1:T(8,128)(2,1)S(1)}, u32[]{:S(2)}, u32[]{:S(2)}) collective-permute-start(bf16[32,8,1,256]{3,0,2,1:T(8,128)(2,1)S(1)} %get-tuple-element.6), channel_id=1, source_target_pairs={{1,0},{2,1},{3,2},{4,3},{5,4},{6,5},{7,6},{9,8},{10,9},{11,10},{12... | collective-permute-start | bytes 393224 | tf_op jit(solution)/shard_map/ppermute | solution.py:15
  63.8 6.7 %copy-start.1 = (bf16[32,8,16,256]{3,0,2,1:T(8,128)(2,1)}, bf16[32,8,16,256]{3,0,2,1:T(8,128)(2,1)S(1)}, u32[]{:S(2)}) copy-start(bf16[32,8,16,256]{3,0,2,1:T(8,128)(2,1)S(1)} %fusion.38) | copy-start | bytes 6291460
  63.8 6.7 %copy-start.6 = (bf16[64,32,2,2]{0,3,2,1:T(2,128)(2,1)S(1)}, bf16[64,32,2,2]{0,3,2,1:T(2,128)(2,1)}, u32[]{:S(2)}) copy-start(bf16[64,32,2,2]{0,3,2,1:T(2,128)(2,1)} %param.12) | copy-start | bytes 49156
  70.5 11.6 %copy-start.3 = (bf16[64,64,3,3,3]{1,0,4,3,2:T(8,128)(2,1)S(1)}, bf16[64,64,3,3,3]{1,0,4,3,2:T(8,128)(2,1)}, u32[]{:S(2)}) copy-start(bf16[64,64,3,3,3]{1,0,4,3,2:T(8,128)(2,1)} %param.13) | copy-start | bytes 663556
  76.8 7.0 %collective-permute-start.4 = (bf16[64,1,8,128]{3,0,2,1:T(8,128)(2,1)S(1)}, bf16[64,1,8,128]{3,0,2,1:T(8,128)(2,1)S(1)}, u32[]{:S(2)}, u32[]{:S(2)}) collective-permute-start(bf16[64,1,8,128]{3,0,2,1:T(8,128)(2,1)S(1)} %get-tuple-element.11), channel_id=1, source_target_pairs={{0,8},{8,16},{16,24},{1,9},{9,17},{17,25},{2,10},{10,18},{18,26},{... | collective-permute-start | bytes 393224 | tf_op jit(solution)/shard_map/ppermute | solution.py:14
  80.0 5.9 %collective-permute-start.5 = (bf16[64,1,8,128]{3,0,2,1:T(8,128)(2,1)S(1)}, bf16[64,1,8,128]{3,0,2,1:T(8,128)(2,1)S(1)}, u32[]{:S(2)}, u32[]{:S(2)}) collective-permute-start(bf16[64,1,8,128]{3,0,2,1:T(8,128)(2,1)S(1)} %get-tuple-element.12), channel_id=1, source_target_pairs={{8,0},{16,8},{24,16},{9,1},{17,9},{25,17},{10,2},{18,10},{26,18},{... | collective-permute-start | bytes 393224 | tf_op jit(solution)/shard_map/ppermute | solution.py:15
  86.0 8.8 %collective-permute-start.6 = (bf16[64,10,1,128]{3,0,2,1:T(8,128)(2,1)S(1)}, bf16[64,10,1,128]{3,0,2,1:T(8,128)(2,1)S(1)}, u32[]{:S(2)}, u32[]{:S(2)}) collective-permute-start(bf16[64,10,1,128]{3,0,2,1:T(8,128)(2,1)S(1)} %get-tuple-element.9), channel_id=1, source_target_pairs={{0,1},{1,2},{2,3},{3,4},{4,5},{5,6},{6,7},{8,9},{9,10},{10,11},{11... | collective-permute-start | bytes 491528 | tf_op jit(solution)/shard_map/ppermute | solution.py:14
  89.4 7.5 %collective-permute-start.7 = (bf16[64,10,1,128]{3,0,2,1:T(8,128)(2,1)S(1)}, bf16[64,10,1,128]{3,0,2,1:T(8,128)(2,1)S(1)}, u32[]{:S(2)}, u32[]{:S(2)}) collective-permute-start(bf16[64,10,1,128]{3,0,2,1:T(8,128)(2,1)S(1)} %get-tuple-element.10), channel_id=1, source_target_pairs={{1,0},{2,1},{3,2},{4,3},{5,4},{6,5},{7,6},{9,8},{10,9},{11,10},{12... | collective-permute-start | bytes 491528 | tf_op jit(solution)/shard_map/ppermute | solution.py:15
  173.7 11.5 %copy-start.2 = (bf16[32,8,16,256]{3,0,2,1:T(8,128)(2,1)S(1)}, bf16[32,8,16,256]{3,0,2,1:T(8,128)(2,1)}, u32[]{:S(2)}) copy-start(bf16[32,8,16,256]{3,0,2,1:T(8,128)(2,1)} %copy-done.1) | copy-start | bytes 6291460
  173.7 11.5 %copy-start.5 = (bf16[3,32]{1,0:T(4,128)(2,1)S(1)}, bf16[3,32]{1,0:T(4,128)(2,1)}, u32[]{:S(2)}) copy-start(bf16[3,32]{1,0:T(4,128)(2,1)} %param.15) | copy-start | bytes 580
where the time goes:
time: 190 us; the launch traced here: 189 us
  matrix products  108 us (57%)
  local copies, waits for them, and re-layouts  36.2 us (19%)
  starting transfers between devices  25.1 us (13%)
  waiting for transfers between devices  11.6 us (6%)
  other arithmetic  7.97 us (4%)
    dot_general x26, matrix products, conv_volume(): jnp.einsum('oc,czxy->ozxy', weights[:, :, offset_z, offset_x, offset_y],...  46.6 us
    dot_general x9, matrix products, conv_plane(): jnp.einsum('oc,czxy->ozxy', weights[:, :, offset_x, offset_y], window, pr...  30.4 us
    dot_general x1, matrix products, per_device(): jnp.einsum('ocab,czxy->ozxayb', w_up, deep, preferred_element_type=jnp.fl...  20.8 us
    ppermute x4, starting transfers between devices, extended(): before = lax.ppermute(last, axis, up)  12.1 us
    reshape x1, local copies, waits for them, and re-layouts, per_device(): raised = raised.reshape(channels, depth_z, width_x, length_y)  11.5 us
    transpose x1, local copies, waits for them, and re-layouts, per_device(): jnp.einsum('ocab,czxy->ozxayb', w_up, deep, preferred_element_type=jnp.fl...  11 us
    ppermute x4, waiting for transfers between devices, extended(): after = lax.ppermute(leading, axis, down)  9.95 us
    ppermute x4, starting transfers between devices, extended(): after = lax.ppermute(leading, axis, down)  8.49 us
  transfers between devices with their start and end apart: 9, of which 5 were waited for; matrix products, arithmetic and copies ran while one was open for 5% of the time, Pallas kernels for 0%

commit v1 on v0

--- a/solution.py
+++ b/solution.py
@@ -67,7 +67,10 @@
 
 
 def per_device(raw, tissue, w_emb, w_one, w_down, w_deep, w_up, w_out):
-    sections = lax.all_to_all(raw, "blk", split_axis=1, concat_axis=0, tiled=True)
+    devices = lax.axis_size("blk")
+    blocks = jnp.stack(jnp.split(raw, devices, axis=1), axis=0)
+    blocks = lax.all_to_all(blocks, "blk", split_axis=0, concat_axis=0)
+    sections = jnp.concatenate(blocks, axis=0)
     depth_z, width_x, length_y = sections.shape
     blocks_y = tissue.shape[2]
     span_y = length_y // blocks_y

time: 190 us -> 197 us (1.037)
  local copies, waits for them, and re-layouts: 36.2 us -> 44.4 us
    unnamed x19 -> x21, local copies, waits for them, and re-layouts: 2.22 us -> 9.1 us
where the time goes in v1:
time: 197 us; the launch traced here: 196 us
  matrix products  108 us (55%)
  local copies, waits for them, and re-layouts  44.4 us (23%)
  starting transfers between devices  25.1 us (13%)
  waiting for transfers between devices  11.6 us (6%)
  other arithmetic  6.96 us (4%)
    dot_general x26, matrix products, conv_volume(): jnp.einsum('oc,czxy->ozxy', weights[:, :, offset_z, offset_x, offset_y],...  46.7 us
    dot_general x9, matrix products, conv_plane(): jnp.einsum('oc,czxy->ozxy', weights[:, :, offset_x, offset_y], window, pr...  30.4 us
    dot_general x1, matrix products, per_device(): jnp.einsum('ocab,czxy->ozxayb', w_up, deep, preferred_element_type=jnp.fl...  20.8 us
    ppermute x4, starting transfers between devices, extended(): before = lax.ppermute(last, axis, up)  12.1 us
    reshape x1, local copies, waits for them, and re-layouts, per_device(): raised = raised.reshape(channels, depth_z, width_x, length_y)  11.6 us
    transpose x1, local copies, waits for them, and re-layouts, per_device(): jnp.einsum('ocab,czxy->ozxayb', w_up, deep, preferred_element_type=jnp.fl...  11 us
    ppermute x4, waiting for transfers between devices, extended(): after = lax.ppermute(leading, axis, down)  9.93 us
    unnamed x21, local copies, waits for them, and re-layouts  9.1 us
  transfers between devices with their start and end apart: 9, of which 5 were waited for; matrix products, arithmetic and copies ran while one was open for 5% of the time, Pallas kernels for 0%

profile of v1, /device:TPU:11, one launch (start us, length us, event | category | flops | bytes accessed | tf_op | source)
XLA Modules:
  0.0 196.2 jit_solution(9240552829451813618)
XLA Ops:
  10.4 4.6 %all-to-all-start = ((bf16[8,1,16,256]{3,2,1,0:T(8,128)(2,1)}), bf16[8,1,16,256]{3,2,1,0:T(8,128)(2,1)S(1)}, u32[]{:S(2)}, u32[]{:S(2)}) async-start(bf16[8,1,16,256]{3,2,1,0:T(8,128)(2,1)} %constant_dynamic-update-slice_fusion), calls=%async_computation | async-start | bytes 131072 | tf_op jit(solution)/shard_map/all_to_all | solution.py:72
  18.3 3.5 %collective-permute-start = (bf16[8,1,256]{2,1,0:T(2,128)(2,1)S(1)}, bf16[8,1,256]{2,1,0:T(2,128)(2,1)S(1)}, u32[]{:S(2)}, u32[]{:S(2)}) collective-permute-start(bf16[8,1,256]{2,1,0:T(2,128)(2,1)S(1)} %get-tuple-element.21), channel_id=1, source_target_pairs={{0,1},{1,2},{2,3},{3,4},{4,5},{5,6},{6,7},{8,9},{9,10},{10,11},{11... | collective-permute-start | bytes 12296 | tf_op jit(solution)/shard_map/ppermute | solution.py:14
  24.0 3.8 %collective-permute-done.1 = bf16[8,1,256]{2,1,0:T(2,128)(2,1)S(1)} collective-permute-done((bf16[8,1,256]{2,1,0:T(2,128)(2,1)S(1)}, bf16[8,1,256]{2,1,0:T(2,128)(2,1)S(1)}, u32[]{:S(2)}, u32[]{:S(2)}) %collective-permute-start.1) | collective-permute-done | bytes 4128 | tf_op jit(solution)/shard_map/ppermute | solution.py:15
  33.6 2.6 %collective-permute-start.3 = (bf16[32,8,1,256]{3,0,2,1:T(8,128)(2,1)S(1)}, bf16[32,8,1,256]{3,0,2,1:T(8,128)(2,1)S(1)}, u32[]{:S(2)}, u32[]{:S(2)}) collective-permute-start(bf16[32,8,1,256]{3,0,2,1:T(8,128)(2,1)S(1)} %get-tuple-element.6), channel_id=1, source_target_pairs={{1,0},{2,1},{3,2},{4,3},{5,4},{6,5},{7,6},{9,8},{10,9},{11,10},{12... | collective-permute-start | bytes 393224 | tf_op jit(solution)/shard_map/ppermute | solution.py:15
  36.2 2.6 %fusion.175 = f32[8,16,256,32]{2,3,1,0:T(8,128)} fusion(bf16[32,8,16,256]{3,0,2,1:T(8,128)(2,1)S(1)} %fusion.41, bf16[32,32,3,3]{1,0,3,2:T(8,128)(2,1)S(1)} %copy-done.4), kind=kOutput, calls=%fused_computation.214 | convolution fusion | flops 67108864 | bytes 6299648 | tf_op jit(solution)/shard_map/oc,czxy->ozxy/dot_general | solution.py:38
  40.8 2.4 %fusion.8 = bf16[32,8,18,258]{3,0,2,1:T(8,128)(2,1)S(1)} fusion(bf16[32,8,1,256]{3,0,2,1:T(8,128)(2,1)S(1)} %collective-permute-done.3, bf16[32,8,16,256]{3,0,2,1:T(8,128)(2,1)S(1)} %fusion.41, bf16[32,8,1,256]{3,0,2,1:T(8,128)(2,1)S(1)} %collective-permute-done.2), kind=kLoop, calls=%fused_computation.15 | loop fusion | flops 14266368 | bytes 4737024 | tf_op jit(solution)/shard_map/concatenate | solution.py:16
  43.2 2.7 %fusion.20 = f32[8,16,256,32]{2,3,1,0:T(8,128)} fusion(bf16[32,8,18,258]{3,0,2,1:T(8,128)(2,1)S(1)} %fusion.8, bf16[32,32,3,3]{1,0,3,2:T(8,128)(2,1)S(1)} %copy-done.4), kind=kOutput, calls=%fused_computation.29 | convolution fusion | flops 67108864 | bytes 6299648 | tf_op jit(solution)/shard_map/oc,czxy->ozxy/dot_general | solution.py:38
  45.9 2.8 %fusion.22 = f32[8,16,256,32]{2,3,1,0:T(8,128)} fusion(bf16[32,8,18,258]{3,0,2,1:T(8,128)(2,1)S(1)} %fusion.8, bf16[32,32,3,3]{1,0,3,2:T(8,128)(2,1)S(1)} %copy-done.4), kind=kOutput, calls=%fused_computation.31 | convolution fusion | flops 67108864 | bytes 6299648 | tf_op jit(solution)/shard_map/oc,czxy->ozxy/dot_general | solution.py:38
  48.7 2.6 %fusion.24 = f32[8,16,256,32]{2,3,1,0:T(8,128)} fusion(bf16[32,8,18,258]{3,0,2,1:T(8,128)(2,1)S(1)} %fusion.8, bf16[32,32,3,3]{1,0,3,2:T(8,128)(2,1)S(1)} %copy-done.4), kind=kOutput, calls=%fused_computation.33 | convolution fusion | flops 67108864 | bytes 6299648 | tf_op jit(solution)/shard_map/oc,czxy->ozxy/dot_general | solution.py:38
  51.3 2.8 %fusion.26 = f32[8,16,256,32]{2,3,1,0:T(8,128)} fusion(bf16[32,8,18,258]{3,0,2,1:T(8,128)(2,1)S(1)} %fusion.8, bf16[32,32,3,3]{1,0,3,2:T(8,128)(2,1)S(1)} %copy-done.4), kind=kOutput, calls=%fused_computation.35 | convolution fusion | flops 67108864 | bytes 6299648 | tf_op jit(solution)/shard_map/oc,czxy->ozxy/dot_general | solution.py:38
  54.1 2.7 %fusion.30 = f32[8,16,256,32]{2,3,1,0:T(8,128)} fusion(bf16[32,8,18,258]{3,0,2,1:T(8,128)(2,1)S(1)} %fusion.8, bf16[32,32,3,3]{1,0,3,2:T(8,128)(2,1)S(1)} %copy-done.4), kind=kOutput, calls=%fused_computation.40 | convolution fusion | flops 67108864 | bytes 6299648 | tf_op jit(solution)/shard_map/oc,czxy->ozxy/dot_general | solution.py:38
  57.5 2.6 %fusion.18 = f32[8,16,256,32]{2,3,1,0:T(8,128)} fusion(bf16[32,8,1,256]{3,0,2,1:T(8,128)(2,1)S(1)} %collective-permute-done.3, bf16[32,8,16,256]{3,0,2,1:T(8,128)(2,1)S(1)} %fusion.41, bf16[32,32,3,3]{1,0,3,2:T(8,128)(2,1)S(1)} %copy-done.4), kind=kOutput, calls=%fused_computation.27 | convolution fusion | flops 71303168 | bytes 6430720 | tf_op jit(solution)/shard_map/oc,czxy->ozxy/dot_general | solution.py:38
  60.1 10.9 %fusion.38 = bf16[32,8,16,256]{3,0,2,1:T(8,128)(2,1)S(1)} fusion(f32[256]{0:T(256)S(1)} %reshape.33, bf16[32,8,18,258]{3,0,2,1:T(8,128)(2,1)S(1)} %fusion.8, f32[8,16,256,32]{2,3,1,0:T(8,128)} %fusion.18, f32[8,16,256,32]{2,3,1,0:T(8,128)} %fusion.20, f32[8,16,256,32]{2,3,1,0:T(8,128)} %fusion.22, f32[8,16,256,32]{2,3,1,0:T(8,128)} %fusion.175, ...), kind=kOutput, calls=%fused_computation.59 | convolution fusion | flops 78643200 | bytes 37757952 | tf_op jit(solution)/shard_map/oc,czxy->ozxy/dot_general | solution.py:38
  71.0 6.7 %copy.167 = bf16[32,8,16,256]{0,1,3,2:T(8,128)(2,1)} copy(bf16[32,8,16,256]{3,0,2,1:T(8,128)(2,1)S(1)} %fusion.38) | data formatting | bytes 4194304 | tf_op jit(solution)/shard_map/convert_element_type | solution.py:91
  77.7 6.3 %fusion.45 = bf16[64,8,8,128]{3,0,2,1:T(8,128)(2,1)S(1)} fusion(bf16[32,8,8,2,128,2]{0,1,5,4,3,2:T(8,128)(2,1)} %bitcast.407, f32[128]{0:T(128)S(1)} %mul.67, bf16[64,32,2,2,1,1]{0,3,2,1,5,4:T(2,128)(2,1)S(1)} %bitcast.409), kind=kOutput, calls=%fused_computation.64 | convolution fusion | flops 135790592 | bytes 3162624 | tf_op jit(solution)/shard_map/ocab,czxayb->ozxy/dot_general | solution.py:93
  84.0 3.2 %collective-permute-start.4 = (bf16[64,1,8,128]{3,0,2,1:T(8,128)(2,1)S(1)}, bf16[64,1,8,128]{3,0,2,1:T(8,128)(2,1)S(1)}, u32[]{:S(2)}, u32[]{:S(2)}) collective-permute-start(bf16[64,1,8,128]{3,0,2,1:T(8,128)(2,1)S(1)} %get-tuple-element.11), channel_id=1, source_target_pairs={{0,8},{8,16},{16,24},{1,9},{9,17},{17,25},{2,10},{10,18},{18,26},{... | collective-permute-start | bytes 393224 | tf_op jit(solution)/shard_map/ppermute | solution.py:14
  91.0 2.1 %collective-permute-done.5 = bf16[64,1,8,128]{3,0,2,1:T(8,128)(2,1)S(1)} collective-permute-done((bf16[64,1,8,128]{3,0,2,1:T(8,128)(2,1)S(1)}, bf16[64,1,8,128]{3,0,2,1:T(8,128)(2,1)S(1)}, u32[]{:S(2)}, u32[]{:S(2)}) %collective-permute-start.5) | collective-permute-done | bytes 131104 | tf_op jit(solution)/shard_map/ppermute | solution.py:15
  93.2 3.4 %collective-permute-start.6 = (bf16[64,10,1,128]{3,0,2,1:T(8,128)(2,1)S(1)}, bf16[64,10,1,128]{3,0,2,1:T(8,128)(2,1)S(1)}, u32[]{:S(2)}, u32[]{:S(2)}) collective-permute-start(bf16[64,10,1,128]{3,0,2,1:T(8,128)(2,1)S(1)} %get-tuple-element.9), channel_id=1, source_target_pairs={{0,1},{1,2},{2,3},{3,4},{4,5},{5,6},{6,7},{8,9},{9,10},{10,11},{11... | collective-permute-start | bytes 491528 | tf_op jit(solution)/shard_map/ppermute | solution.py:14
  102.0 2.1 %collective-permute-done.7 = bf16[64,10,1,128]{3,0,2,1:T(8,128)(2,1)S(1)} collective-permute-done((bf16[64,10,1,128]{3,0,2,1:T(8,128)(2,1)S(1)}, bf16[64,10,1,128]{3,0,2,1:T(8,128)(2,1)S(1)}, u32[]{:S(2)}, u32[]{:S(2)}) %collective-permute-start.7) | collective-permute-done | bytes 163872 | tf_op jit(solution)/shard_map/ppermute | solution.py:15
  104.1 3.1 %select_maximum_fusion = bf16[64,10,10,130]{3,0,2,1:T(8,128)(2,1)S(1)} fusion(bf16[64,10,1,128]{3,0,2,1:T(8,128)(2,1)S(1)} %collective-permute-done.7, bf16[64,10,1,128]{3,0,2,1:T(8,128)(2,1)S(1)} %collective-permute-done.6, bf16[64,1,8,128]{3,0,2,1:T(8,128)(2,1)S(1)} %collective-permute-done.5, bf16[64,8,8,128]{3,0,2,1:T(8,128)(2,1)S(1)} %fusion.45, ...), kind=kLoop, calls=%fused_computation.16 | loop fusion | flops 14976000 | bytes 3302400 | tf_op jit(solution)/shard_map/concatenate | solution.py:16
  149.1 20.8 %convolution_bitcast_fusion = f32[32,8,8,2,128,2]{4,0,5,3,2,1:T(8,128)} fusion(f32[8,8,128,64]{2,3,1,0:T(8,128)} %fusion.52, f32[8,8,128,64]{2,3,1,0:T(8,128)} %fusion.54, f32[8,8,128,64]{2,3,1,0:T(8,128)} %fusion.56, f32[8,8,128,64]{2,3,1,0:T(8,128)} %fusion.58, f32[8,8,128,64]{2,3,1,0:T(8,128)} %fusion.60, f32[8,8,128,64]{2,3,1,0:T(8,128)} %fusion.62, ...), kind=kOutput, calls=%fused_computation.23 | convolution fusion | flops 216530944 | bytes 59818496 | tf_op jit(solution)/shard_map/ocab,czxy->ozxayb/dot_general | solution.py:99
  169.9 11.0 %copy.171 = f32[32,8,8,2,128,2]{0,1,5,4,3,2:T(8,128)} copy(f32[32,8,8,2,128,2]{4,0,5,3,2,1:T(8,128)} %convolution_bitcast_fusion) | data formatting | bytes 8388608 | tf_op jit(solution)/shard_map/ocab,czxy->ozxayb/transpose | solution.py:99
  180.9 11.6 %copy.172 = f32[32,8,16,256]{3,0,2,1:T(8,128)} copy(f32[32,8,16,256]{0,1,3,2:T(8,128)} %bitcast.406) | data formatting | bytes 8388608 | tf_op jit(solution)/shard_map/reshape | solution.py:100
  192.5 2.9 %fusion.49 = f32[3,8,16,256]{3,0,2,1:T(4,128)S(1)} fusion(f32[32,8,16,256]{3,0,2,1:T(8,128)} %copy.172, bf16[32,8,16,256]{3,0,2,1:T(8,128)(2,1)S(1)} %copy-done.2, f32[256]{0:T(256)S(1)} %reshape.33, bf16[3,32]{1,0:T(4,128)(2,1)S(1)} %copy-done.5), kind=kOutput, calls=%fused_computation.66 | convolution fusion | flops 11632640 | bytes 6685888 | tf_op jit(solution)/shard_map/oc,czxy->ozxy/dot_general | solution.py:104
  (87 shorter events, 76.3 us)
Async XLA Ops:
  0.0 149.1 %copy-start = (bf16[32,64,2,2]{1,3,2,0:T(2,128)(2,1)S(1)}, bf16[32,64,2,2]{1,3,2,0:T(2,128)(2,1)}, u32[]{:S(2)}) copy-start(bf16[32,64,2,2]{1,3,2,0:T(2,128)(2,1)} %param.14) | copy-start | bytes 49156
  10.4 7.9 %all-to-all-start = ((bf16[8,1,16,256]{3,2,1,0:T(8,128)(2,1)}), bf16[8,1,16,256]{3,2,1,0:T(8,128)(2,1)S(1)}, u32[]{:S(2)}, u32[]{:S(2)}) async-start(bf16[8,1,16,256]{3,2,1,0:T(8,128)(2,1)} %constant_dynamic-update-slice_fusion), calls=%async_computation | async-start | bytes 131072 | tf_op jit(solution)/shard_map/all_to_all | solution.py:72
  18.3 5.6 %collective-permute-start = (bf16[8,1,256]{2,1,0:T(2,128)(2,1)S(1)}, bf16[8,1,256]{2,1,0:T(2,128)(2,1)S(1)}, u32[]{:S(2)}, u32[]{:S(2)}) collective-permute-start(bf16[8,1,256]{2,1,0:T(2,128)(2,1)S(1)} %get-tuple-element.21), channel_id=1, source_target_pairs={{0,1},{1,2},{2,3},{3,4},{4,5},{5,6},{6,7},{8,9},{9,10},{10,11},{11... | collective-permute-start | bytes 12296 | tf_op jit(solution)/shard_map/ppermute | solution.py:14
  21.9 5.9 %collective-permute-start.1 = (bf16[8,1,256]{2,1,0:T(2,128)(2,1)S(1)}, bf16[8,1,256]{2,1,0:T(2,128)(2,1)S(1)}, u32[]{:S(2)}, u32[]{:S(2)}) collective-permute-start(bf16[8,1,256]{2,1,0:T(2,128)(2,1)S(1)} %get-tuple-element.22), channel_id=1, source_target_pairs={{1,0},{2,1},{3,2},{4,3},{5,4},{6,5},{7,6},{9,8},{10,9},{11,10},{12... | collective-permute-start | bytes 12296 | tf_op jit(solution)/shard_map/ppermute | solution.py:15
  30.9 5.3 %copy-start.4 = (bf16[32,32,3,3]{1,0,3,2:T(8,128)(2,1)S(1)}, bf16[32,32,3,3]{1,0,3,2:T(8,128)(2,1)}, u32[]{:S(2)}) copy-start(bf16[32,32,3,3]{1,0,3,2:T(8,128)(2,1)} %param.11) | copy-start | bytes 55300
  31.7 7.2 %collective-permute-start.2 = (bf16[32,8,1,256]{3,0,2,1:T(8,128)(2,1)S(1)}, bf16[32,8,1,256]{3,0,2,1:T(8,128)(2,1)S(1)}, u32[]{:S(2)}, u32[]{:S(2)}) collective-permute-start(bf16[32,8,1,256]{3,0,2,1:T(8,128)(2,1)S(1)} %get-tuple-element.5), channel_id=1, source_target_pairs={{0,1},{1,2},{2,3},{3,4},{4,5},{5,6},{6,7},{8,9},{9,10},{10,11},{11... | collective-permute-start | bytes 393224 | tf_op jit(solution)/shard_map/ppermute | solution.py:14
  33.6 7.2 %collective-permute-start.3 = (bf16[32,8,1,256]{3,0,2,1:T(8,128)(2,1)S(1)}, bf16[32,8,1,256]{3,0,2,1:T(8,128)(2,1)S(1)}, u32[]{:S(2)}, u32[]{:S(2)}) collective-permute-start(bf16[32,8,1,256]{3,0,2,1:T(8,128)(2,1)S(1)} %get-tuple-element.6), channel_id=1, source_target_pairs={{1,0},{2,1},{3,2},{4,3},{5,4},{6,5},{7,6},{9,8},{10,9},{11,10},{12... | collective-permute-start | bytes 393224 | tf_op jit(solution)/shard_map/ppermute | solution.py:15
  71.0 6.7 %copy-start.1 = (bf16[32,8,16,256]{3,0,2,1:T(8,128)(2,1)}, bf16[32,8,16,256]{3,0,2,1:T(8,128)(2,1)S(1)}, u32[]{:S(2)}) copy-start(bf16[32,8,16,256]{3,0,2,1:T(8,128)(2,1)S(1)} %fusion.38) | copy-start | bytes 6291460
  71.0 6.7 %copy-start.6 = (bf16[64,32,2,2]{0,3,2,1:T(2,128)(2,1)S(1)}, bf16[64,32,2,2]{0,3,2,1:T(2,128)(2,1)}, u32[]{:S(2)}) copy-start(bf16[64,32,2,2]{0,3,2,1:T(2,128)(2,1)} %param.12) | copy-start | bytes 49156
  77.7 11.6 %copy-start.3 = (bf16[64,64,3,3,3]{1,0,4,3,2:T(8,128)(2,1)S(1)}, bf16[64,64,3,3,3]{1,0,4,3,2:T(8,128)(2,1)}, u32[]{:S(2)}) copy-start(bf16[64,64,3,3,3]{1,0,4,3,2:T(8,128)(2,1)} %param.13) | copy-start | bytes 663556
  84.0 7.0 %collective-permute-start.4 = (bf16[64,1,8,128]{3,0,2,1:T(8,128)(2,1)S(1)}, bf16[64,1,8,128]{3,0,2,1:T(8,128)(2,1)S(1)}, u32[]{:S(2)}, u32[]{:S(2)}) collective-permute-start(bf16[64,1,8,128]{3,0,2,1:T(8,128)(2,1)S(1)} %get-tuple-element.11), channel_id=1, source_target_pairs={{0,8},{8,16},{16,24},{1,9},{9,17},{17,25},{2,10},{10,18},{18,26},{... | collective-permute-start | bytes 393224 | tf_op jit(solution)/shard_map/ppermute | solution.py:14
  87.2 5.9 %collective-permute-start.5 = (bf16[64,1,8,128]{3,0,2,1:T(8,128)(2,1)S(1)}, bf16[64,1,8,128]{3,0,2,1:T(8,128)(2,1)S(1)}, u32[]{:S(2)}, u32[]{:S(2)}) collective-permute-start(bf16[64,1,8,128]{3,0,2,1:T(8,128)(2,1)S(1)} %get-tuple-element.12), channel_id=1, source_target_pairs={{8,0},{16,8},{24,16},{9,1},{17,9},{25,17},{10,2},{18,10},{26,18},{... | collective-permute-start | bytes 393224 | tf_op jit(solution)/shard_map/ppermute | solution.py:15
  93.2 8.8 %collective-permute-start.6 = (bf16[64,10,1,128]{3,0,2,1:T(8,128)(2,1)S(1)}, bf16[64,10,1,128]{3,0,2,1:T(8,128)(2,1)S(1)}, u32[]{:S(2)}, u32[]{:S(2)}) collective-permute-start(bf16[64,10,1,128]{3,0,2,1:T(8,128)(2,1)S(1)} %get-tuple-element.9), channel_id=1, source_target_pairs={{0,1},{1,2},{2,3},{3,4},{4,5},{5,6},{6,7},{8,9},{9,10},{10,11},{11... | collective-permute-start | bytes 491528 | tf_op jit(solution)/shard_map/ppermute | solution.py:14
  96.5 7.5 %collective-permute-start.7 = (bf16[64,10,1,128]{3,0,2,1:T(8,128)(2,1)S(1)}, bf16[64,10,1,128]{3,0,2,1:T(8,128)(2,1)S(1)}, u32[]{:S(2)}, u32[]{:S(2)}) collective-permute-start(bf16[64,10,1,128]{3,0,2,1:T(8,128)(2,1)S(1)} %get-tuple-element.10), channel_id=1, source_target_pairs={{1,0},{2,1},{3,2},{4,3},{5,4},{6,5},{7,6},{9,8},{10,9},{11,10},{12... | collective-permute-start | bytes 491528 | tf_op jit(solution)/shard_map/ppermute | solution.py:15
  180.9 11.6 %copy-start.2 = (bf16[32,8,16,256]{3,0,2,1:T(8,128)(2,1)S(1)}, bf16[32,8,16,256]{3,0,2,1:T(8,128)(2,1)}, u32[]{:S(2)}) copy-start(bf16[32,8,16,256]{3,0,2,1:T(8,128)(2,1)} %copy-done.1) | copy-start | bytes 6291460
  180.9 11.6 %copy-start.5 = (bf16[3,32]{1,0:T(4,128)(2,1)S(1)}, bf16[3,32]{1,0:T(4,128)(2,1)}, u32[]{:S(2)}) copy-start(bf16[3,32]{1,0:T(4,128)(2,1)} %param.15) | copy-start | bytes 580
